TPU v7x, 32 devices: a whole 2x2x4 slice. The times are simulated.
32 devices in a mesh: region: 8 (over z, core), member: 4 (over y, x).
Axes of the slice: x: 2, y: 2, z: 4, core: 2. Of those that a mesh axis runs over, the one named last changes fastest.
Arguments:
- positions: float32 [3, 12288], P(None, ('region', 'member'))
- forces: float32 [3, 12288], P(None, ('region', 'member')), may hold values from -6 to 6
- blob_platelet: int32 [12288], P(('region', 'member')), may hold values from 0 to 8, as said below
- blob_rank: int32 [12288], P(('region', 'member')), may hold values from 0 to 161, as said below
- platelet_owner: int32 [64], P('region'), may hold values from 0 to 7, as said below
- pair_list: int32 [96, 8], P(('region', 'member')), may hold values from 0 to 23, as said below
- pair_count: int32 [96], P(('region', 'member')), may hold values from 1 to 8, as said below
- preconditioner: bfloat16 [64, 486, 486], P(('region', 'member')), may hold values from -0.25 to 0.25
Outputs:
- blob_velocity: float32 [3, 12288], P(None, ('region', 'member'))
- body_velocity: float32 [64, 486], P(('region', 'member'))
Inputs may be any that keep to these rules, and one draw needn't show every extreme that they name: `blob_platelet`: in each slab every platelet id below 8 appears on exactly 162 slots, and 8 marks an empty slot. Every device holds exactly 324 live blobs, of which at most 121 belong to platelets whose owner slots lie on one member; that bound is met in every slab. `blob_rank`: the 162 blobs of one platelet have distinct ranks; empty slots have rank 0. `platelet_owner`: the 8 entries of one slab are a permutation; owner slot o lies on member o // 2 of that slab. `pair_list`: the entries of one target tile are distinct, and entry 0 is the tile itself, 6 plus its index within its slab. `pair_count`: some tile has 8 in every draw.
All inputs are finite; a program needn't handle non-finite values.
Results may differ from a plain program's by a relative error of at most 0.0029.
Values sent between devices are 32-bit elements; how exact they have to be, the bound alone decides.
A program may use at most 64 MiB of HBM per device.

v0:
```python
import math

import jax
import jax.numpy as jnp
from jax import lax
from jax.sharding import PartitionSpec as P

TILE = 128
PB = 162
PLAT_DEV = 2


soft_square = 1.0


def padded(cells, sides, width):
    for axis, dim in sides:
        count = lax.axis_size(axis)
        ends = count - 1
        head = lax.slice_in_dim(cells, 0, width, axis=dim)
        tail = lax.slice_in_dim(cells, cells.shape[dim] - width, cells.shape[dim], axis=dim)
        cells = jnp.concatenate(
            [
                lax.ppermute(tail, axis, [(i, (i + 1) % count) for i in range(ends)]),
                cells,
                lax.ppermute(head, axis, [((i + 1) % count, i) for i in range(ends)]),
            ],
            axis=dim,
        )
    return cells


def stokes_sum(targets, sources, pushes):
    force = pushes[:, :, None, :]
    separation = targets[:, :, :, None] - sources[:, :, None, :]
    dist_square = jnp.sum(separation * separation, axis=0)
    force_along = jnp.sum(separation * force, axis=0)
    kernel_weight = 1.0 / (
        8.0 * math.pi * (dist_square + soft_square) * jnp.sqrt(dist_square + soft_square)
    )
    direct = ((dist_square + 2.0 * soft_square) * force + separation * force_along) * kernel_weight
    flip_source = jnp.array([1.0, 1.0, -1.0], jnp.float32)[:, None, None]
    flip_pair = jnp.array([1.0, 1.0, -1.0], jnp.float32)[:, None, None, None]
    unit_normal = jnp.array([0.0, 0.0, 1.0], jnp.float32)[:, None, None, None]
    height = sources[2][:, None, :]
    image_gap = targets[:, :, :, None] - (sources * flip_source)[:, :, None, :]
    image_square = jnp.sum(image_gap * image_gap, axis=0)
    inverse_one = 1.0 / jnp.sqrt(image_square)
    inverse_three = inverse_one * inverse_one * inverse_one
    inverse_five = inverse_three * inverse_one * inverse_one
    image_along = jnp.sum(image_gap * force, axis=0)
    mirrored = force * flip_pair
    mirror_along = jnp.sum(image_gap * mirrored, axis=0)
    normal_gap = image_gap[2]
    stokes_image = force * inverse_one + image_gap * image_along * inverse_three
    doublet = height * (mirrored * inverse_three - 3.0 * image_gap * mirror_along * inverse_five)
    doublet = doublet + unit_normal * mirror_along * inverse_three
    doublet = doublet - (mirrored * normal_gap + image_gap * mirrored[2]) * inverse_three
    doublet = doublet + 3.0 * image_gap * normal_gap * mirror_along * inverse_five
    wall_term = (2.0 * height * doublet - stokes_image) * (1.0 / (8.0 * math.pi))
    return jnp.sum(direct + wall_term, axis=3)


def on_device(
    positions,
    forces,
    blob_platelet,
    blob_rank,
    platelet_owner,
    pair_list,
    pair_count,
    preconditioner,
):
    blob_count = positions.shape[1]
    plate_count = platelet_owner.shape[0]
    is_live = blob_platelet < plate_count
    live_mask = is_live.astype(jnp.float32)
    own_blobs = jnp.concatenate([positions, forces * live_mask[None, :]], 0)
    region_all = lax.all_gather(own_blobs, "member", axis=1, tiled=True)
    extended = padded(region_all, (("region", 1),), region_all.shape[1] // 2)
    ext_blocks = extended.reshape(6, extended.shape[1] // TILE, TILE)
    targets = positions.reshape(3, blob_count // TILE, TILE)
    pair_rounds = jnp.max(pair_count)

    def one_slot(pair_slot, accumulated):
        source_ids = lax.dynamic_index_in_dim(pair_list, pair_slot, 1, keepdims=False)
        picked = jnp.take(ext_blocks, source_ids, axis=1)
        keep_mask = (pair_slot < pair_count).astype(jnp.float32)
        return accumulated + keep_mask[None, :, None] * stokes_sum(targets, picked[:3], picked[3:])

    velocity = lax.fori_loop(0, pair_rounds, one_slot, jnp.zeros(targets.shape, jnp.float32))
    blob_velocity = velocity.reshape(3, blob_count)
    plate_match = blob_platelet[:, None] == jnp.arange(plate_count, dtype=jnp.int32)[None, :]
    slot_of = jnp.sum(jnp.where(plate_match, platelet_owner[None, :], 0), axis=1)
    whole_body = PLAT_DEV * PB
    region_target = jnp.where(is_live, slot_of * PB + blob_rank, plate_count * PB)
    all_velocity, all_target = (
        lax.all_gather(blob_velocity, "member", axis=1, tiled=True),
        lax.all_gather(region_target, "member", axis=0, tiled=True),
    )
    local_index = all_target - lax.axis_index("member") * whole_body
    local_index = jnp.where(
        (local_index >= 0) & (local_index < whole_body), local_index, whole_body
    )
    body_flat = (
        jnp.zeros((3, whole_body), jnp.float32).at[:, local_index].set(all_velocity, mode="drop")
    )
    body_in = (
        body_flat.reshape(3, PLAT_DEV, PB)
        .transpose(1, 0, 2)
        .reshape(PLAT_DEV, 3 * PB)
        .astype(jnp.bfloat16)
    )
    body_velocity = jnp.einsum(
        "pab,pb->pa", preconditioner, body_in, preferred_element_type=jnp.float32
    )
    return (blob_velocity, body_velocity)


def solution(mesh):
    placed = (
        P(None, ("region", "member")),
        P(None, ("region", "member")),
        P(("region", "member")),
        P(("region", "member")),
        P("region"),
        P(("region", "member"), None),
        P(("region", "member")),
        P(("region", "member"), None, None),
    )
    return jax.shard_map(
        on_device,
        mesh=mesh,
        in_specs=placed,
        out_specs=(P(None, ("region", "member")), P(("region", "member"), None)),
        check_vma=False,
    )
```

profile of v0, /device:TPU:0, one launch (start us, length us, event | category | flops | bytes accessed | tf_op | source)
XLA Modules:
  0.0 66.3 jit_solution(10608921622263139967)
XLA Ops:
  0.7 0.9 %select_reduce_fusion = s32[384]{0:T(512)S(1)} fusion(s32[8]{0:T(128)} %param.17, s32[384]{0:T(512)} %param.15), kind=kLoop, calls=%fused_computation.62 | loop fusion | flops 8832 | bytes 3104 | tf_op jit(solution)/shard_map/reduce_sum | solution.py:94
  1.6 0.7 copy-done.6
  2.2 0.7 %copy-done.1 = f32[3,384]{1,0:T(4,128)S(1)} copy-done((f32[3,384]{1,0:T(4,128)S(1)}, f32[3,384]{1,0:T(4,128)}, u32[]{:S(2)}) %copy-start.1) | copy-done | bytes 4632
  2.9 9.7 %all_gather.9 = f32[6,1536]{1,0:T(8,128)S(1)} all-gather(f32[6,384]{1,0:T(8,128)S(1)} %pad_maximum_fusion), channel_id=1, replica_groups=mesh['region'=8,'member'=4] {'member'}, dimensions={1}, use_global_device_ids=true | all-gather | bytes 46080 | tf_op jit(solution)/shard_map/all_gather | solution.py:79
  12.7 1.3 %collective-permute-start.1 = (f32[6,768]{1,0:T(8,128)S(1)}, f32[6,768]{1,0:T(8,128)S(1)}, u32[]{:S(2)}, u32[]{:S(2)}) collective-permute-start(f32[6,768]{1,0:T(8,128)S(1)} %get-tuple-element.180), channel_id=1, source_target_pairs={{4,0},{8,4},{12,8},{16,12},{20,16},{24,20},{28,24},{5,1},{9,5},{13... | collective-permute-start | bytes 55304 | tf_op jit(solution)/shard_map/ppermute | solution.py:26
  14.0 3.0 %collective-permute-start = (f32[6,768]{1,0:T(8,128)S(1)}, f32[6,768]{1,0:T(8,128)S(1)}, u32[]{:S(2)}, u32[]{:S(2)}) collective-permute-start(f32[6,768]{1,0:T(8,128)S(1)} %get-tuple-element.179), channel_id=1, source_target_pairs={{0,4},{4,8},{8,12},{12,16},{16,20},{20,24},{24,28},{1,5},{5,9},{9,... | collective-permute-start | bytes 55304 | tf_op jit(solution)/shard_map/ppermute | solution.py:24
  17.0 8.1 %all-gather = s32[4,1,384]{2,1,0:T(1,128)S(1)} all-gather(s32[1,1,384]{2,1,0:T(1,128)S(1)} %reshape.93), channel_id=1, replica_groups=mesh['region'=8,'member'=4] {'member'}, dimensions={0}, use_global_device_ids=true | all-gather | bytes 7680 | tf_op jit(solution)/shard_map/all_gather | solution.py:99
  25.2 0.7 copy-done.8
  25.8 0.1 copy.43
  25.9 0.6 copy-done.9
  26.5 0.6 reduce_max.9
  27.2 0.6 copy-done.3
  27.8 19.1 %while.13 = (s32[]{:T(128)}, f32[3,3,128]{2,1,0:T(4,128)S(1)}, s32[]{:T(128)}, s32[3]{0:T(128)S(1)}, f32[3,384]{1,0:T(4,128)}, /*index=5*/s32[3,8]{0,1:T(8,128)S...) while((s32[]{:T(128)}, f32[3,3,128]{2,1,0:T(4,128)S(1)}, ...), condition=%wide.wide.region_8.9_spmd.clone.clone, body=%wide.wide.region_1.8_spmd.sunk.clone.clone.sunk | while | flops 6790173 | bytes 6481697 | solution.py:91
  28.5 0.6 gather_fusion
  29.1 0.1 select_bitcast_fusion.3
  29.1 0.1 broadcast_multiply_fusion.10
  29.2 0.3 fusion.34
  29.7 0.1 broadcast_add_fusion.3
  29.8 1.0 %fusion.35 = f32[3,3,128]{2,1,0:T(4,128)S(1)} fusion(f32[3,128,128]{2,1,0:T(8,128)S(1)} %get-tuple-element.308, f32[3,128,128]{2,1,0:T(8,128)S(1)} %get-tuple-element.311, f32[3,128,128]{2,1,0:T(8,128)S(1)} %get-tuple-element.312, f32[3,128]{1,0:T(4,128)S(1)} %get-tuple-element.313, f32[3,128,128]{2,1,0:T(8,128)S(1)} %slice_bitcast_fusion.3, ...), kind=kLoop, calls=%fused_computation.17.clone.clone.1 | loop fusion | flops 4717440 | bytes 2194956 | tf_op jit(solution)/shard_map/while/body/reduce_sum | solution.py:61
  30.8 0.1 multiply_add_fusion.3
  31.6 0.6 gather_fusion
  32.1 0.1 select_bitcast_fusion.3
  32.2 0.1 broadcast_multiply_fusion.10
  32.3 0.3 fusion.34
  32.6 0.1 multiply_multiply_fusion.4
  32.7 0.1 broadcast_add_fusion.3
  32.9 1.0 %fusion.35 = f32[3,3,128]{2,1,0:T(4,128)S(1)} fusion(f32[3,128,128]{2,1,0:T(8,128)S(1)} %get-tuple-element.308, f32[3,128,128]{2,1,0:T(8,128)S(1)} %get-tuple-element.311, f32[3,128,128]{2,1,0:T(8,128)S(1)} %get-tuple-element.312, f32[3,128]{1,0:T(4,128)S(1)} %get-tuple-element.313, f32[3,128,128]{2,1,0:T(8,128)S(1)} %slice_bitcast_fusion.3, ...), kind=kLoop, calls=%fused_computation.17.clone.clone.1 | loop fusion | flops 4717440 | bytes 2194956 | tf_op jit(solution)/shard_map/while/body/reduce_sum | solution.py:61
  33.9 0.1 multiply_add_fusion.3
  34.7 0.6 gather_fusion
  35.2 0.1 select_bitcast_fusion.3
  35.3 0.1 broadcast_multiply_fusion.10
  35.4 0.3 fusion.34
  35.8 0.1 broadcast_add_fusion.3
  35.9 1.0 %fusion.35 = f32[3,3,128]{2,1,0:T(4,128)S(1)} fusion(f32[3,128,128]{2,1,0:T(8,128)S(1)} %get-tuple-element.308, f32[3,128,128]{2,1,0:T(8,128)S(1)} %get-tuple-element.311, f32[3,128,128]{2,1,0:T(8,128)S(1)} %get-tuple-element.312, f32[3,128]{1,0:T(4,128)S(1)} %get-tuple-element.313, f32[3,128,128]{2,1,0:T(8,128)S(1)} %slice_bitcast_fusion.3, ...), kind=kLoop, calls=%fused_computation.17.clone.clone.1 | loop fusion | flops 4717440 | bytes 2194956 | tf_op jit(solution)/shard_map/while/body/reduce_sum | solution.py:61
  37.0 0.1 multiply_add_fusion.3
  37.7 0.6 gather_fusion
  38.3 0.1 select_bitcast_fusion.3
  38.4 0.1 broadcast_multiply_fusion.10
  38.5 0.3 fusion.34
  38.9 0.1 broadcast_add_fusion.3
  39.0 1.0 %fusion.35 = f32[3,3,128]{2,1,0:T(4,128)S(1)} fusion(f32[3,128,128]{2,1,0:T(8,128)S(1)} %get-tuple-element.308, f32[3,128,128]{2,1,0:T(8,128)S(1)} %get-tuple-element.311, f32[3,128,128]{2,1,0:T(8,128)S(1)} %get-tuple-element.312, f32[3,128]{1,0:T(4,128)S(1)} %get-tuple-element.313, f32[3,128,128]{2,1,0:T(8,128)S(1)} %slice_bitcast_fusion.3, ...), kind=kLoop, calls=%fused_computation.17.clone.clone.1 | loop fusion | flops 4717440 | bytes 2194956 | tf_op jit(solution)/shard_map/while/body/reduce_sum | solution.py:61
  40.0 0.1 multiply_add_fusion.3
  40.8 0.6 gather_fusion
  41.4 0.1 select_bitcast_fusion.3
  41.5 0.1 broadcast_multiply_fusion.10
  41.6 0.3 fusion.34
  42.0 0.1 broadcast_add_fusion.3
  42.1 1.0 %fusion.35 = f32[3,3,128]{2,1,0:T(4,128)S(1)} fusion(f32[3,128,128]{2,1,0:T(8,128)S(1)} %get-tuple-element.308, f32[3,128,128]{2,1,0:T(8,128)S(1)} %get-tuple-element.311, f32[3,128,128]{2,1,0:T(8,128)S(1)} %get-tuple-element.312, f32[3,128]{1,0:T(4,128)S(1)} %get-tuple-element.313, f32[3,128,128]{2,1,0:T(8,128)S(1)} %slice_bitcast_fusion.3, ...), kind=kLoop, calls=%fused_computation.17.clone.clone.1 | loop fusion | flops 4717440 | bytes 2194956 | tf_op jit(solution)/shard_map/while/body/reduce_sum | solution.py:61
  43.1 0.1 multiply_add_fusion.3
  43.9 0.6 gather_fusion
  44.5 0.1 select_bitcast_fusion.3
  44.5 0.1 broadcast_multiply_fusion.10
  44.6 0.3 fusion.34
  45.1 0.1 broadcast_add_fusion.3
  45.2 1.0 %fusion.35 = f32[3,3,128]{2,1,0:T(4,128)S(1)} fusion(f32[3,128,128]{2,1,0:T(8,128)S(1)} %get-tuple-element.308, f32[3,128,128]{2,1,0:T(8,128)S(1)} %get-tuple-element.311, f32[3,128,128]{2,1,0:T(8,128)S(1)} %get-tuple-element.312, f32[3,128]{1,0:T(4,128)S(1)} %get-tuple-element.313, f32[3,128,128]{2,1,0:T(8,128)S(1)} %slice_bitcast_fusion.3, ...), kind=kLoop, calls=%fused_computation.17.clone.clone.1 | loop fusion | flops 4717440 | bytes 2194956 | tf_op jit(solution)/shard_map/while/body/reduce_sum | solution.py:61
  46.2 0.1 multiply_add_fusion.3
  47.0 13.4 %all_gather.11 = f32[3,1536]{1,0:T(4,128)S(1)} all-gather(f32[3,384]{1,0:T(4,128)S(1)} %bitcast.48), channel_id=1, replica_groups=mesh['region'=8,'member'=4] {'member'}, dimensions={1}, use_global_device_ids=true | all-gather | bytes 23040 | tf_op jit(solution)/shard_map/all_gather | solution.py:98
  60.4 0.3 copy.44
  60.7 4.4 %scatter_custom_fusion = f32[3,324]{0,1:T(8,128)S(1)} fusion(s32[1536]{0:T(1024)S(1)} %compare_select_fusion.1, f32[1536,3]{1,0:T(8,128)S(1)} %copy.44, f32[]{:T(128)} %constant.14.clone.1), kind=kCustom, calls=%fused_computation.58 | custom fusion | bytes 3892 | tf_op jit(solution)/shard_map/scatter | solution.py:106
  65.0 0.1 copy.53
  65.1 0.1 convert_element_type.24
  65.2 0.1 reshape.100
  65.3 0.4 fusion.24
  65.7 0.6 copy.63
  (109 shorter events, 0.9 us)
Async XLA Ops:
  0.6 64.7 %copy-start = (bf16[2,486,486]{2,0,1:T(2,128)(2,1)S(1)}, bf16[2,486,486]{2,0,1:T(2,128)(2,1)}, u32[]{:S(2)}) copy-start(bf16[2,486,486]{2,0,1:T(2,128)(2,1)} %param.20) | copy-start | bytes 2834356
  0.6 0.9 %copy-start.5 = (s32[384]{0:T(512)S(1)}, s32[384]{0:T(512)}, u32[]{:S(2)}) copy-start(s32[384]{0:T(512)} %param.15) | copy-start | bytes 4612
  0.7 0.9 %copy-start.7 = (s32[384]{0:T(512)S(1)}, s32[384]{0:T(512)}, u32[]{:S(2)}) copy-start(s32[384]{0:T(512)} %param.16) | copy-start | bytes 4612
  1.5 0.7 %copy-start.6 = (f32[3,384]{1,0:T(4,128)S(1)}, f32[3,384]{1,0:T(4,128)}, u32[]{:S(2)}) copy-start(f32[3,384]{1,0:T(4,128)} %param.14) | copy-start | bytes 13828
  2.2 0.7 %copy-start.1 = (f32[3,384]{1,0:T(4,128)S(1)}, f32[3,384]{1,0:T(4,128)}, u32[]{:S(2)}) copy-start(f32[3,384]{1,0:T(4,128)} %param.13) | copy-start | bytes 13828
  12.7 14.5 %collective-permute-start.1 = (f32[6,768]{1,0:T(8,128)S(1)}, f32[6,768]{1,0:T(8,128)S(1)}, u32[]{:S(2)}, u32[]{:S(2)}) collective-permute-start(f32[6,768]{1,0:T(8,128)S(1)} %get-tuple-element.180), channel_id=1, source_target_pairs={{4,0},{8,4},{12,8},{16,12},{20,16},{24,20},{28,24},{5,1},{9,5},{13... | collective-permute-start | bytes 55304 | tf_op jit(solution)/shard_map/ppermute | solution.py:26
  14.0 13.2 %collective-permute-start = (f32[6,768]{1,0:T(8,128)S(1)}, f32[6,768]{1,0:T(8,128)S(1)}, u32[]{:S(2)}, u32[]{:S(2)}) collective-permute-start(f32[6,768]{1,0:T(8,128)S(1)} %get-tuple-element.179), channel_id=1, source_target_pairs={{0,4},{4,8},{8,12},{12,16},{16,20},{20,24},{24,28},{1,5},{5,9},{9,... | collective-permute-start | bytes 55304 | tf_op jit(solution)/shard_map/ppermute | solution.py:24
  25.1 0.7 %copy-start.8 = (s32[3,8]{1,0:T(4,128)S(1)}, s32[3,8]{1,0:T(4,128)}, u32[]{:S(2)}) copy-start(s32[3,8]{1,0:T(4,128)} %param.18) | copy-start | bytes 292
  25.8 0.7 copy-start.9
  27.1 0.7 copy-start.3
  27.1 0.7 copy-start.4
  47.0 13.4 %copy-start.2 = (f32[1,3,3,128]{3,1,2,0:T(4,128)}, f32[1,3,3,128]{3,1,2,0:T(4,128)S(1)}, u32[]{:S(2)}) copy-start(f32[1,3,3,128]{3,1,2,0:T(4,128)S(1)} %copy.62) | copy-start | bytes 13828
where the time goes:
time: 66.8 us; the launch traced here: 66.3 us
  blocking collectives  31.2 us (47%)
  local copies, waits for them, and re-layouts  12.4 us (19%)
  other arithmetic  11.9 us (18%)
  loops' own time  5.28 us (8%)
  starting transfers between devices  4.32 us (6%)
  between operations  0.83 us (1%)
    all_gather x1, blocking collectives, on_device(): lax.all_gather(blob_velocity, 'member', axis=1, tiled=True)  13.4 us
    all_gather x1, blocking collectives, on_device(): region_all = lax.all_gather(own_blobs, 'member', axis=1, tiled=True)  9.71 us
    all_gather x1, blocking collectives, on_device(): lax.all_gather(region_target, 'member', axis=0, tiled=True)  8.06 us
    reduce_sum x6, other arithmetic, stokes_sum(): return jnp.sum(direct + wall_term, axis=3)  6.11 us
    another operation x1, loops' own time, on_device(): lax.fori_loop(0, pair_rounds, one_slot, jnp.zeros(targets.shape, jnp.floa...  5.28 us
    scatter x1, local copies, waits for them, and re-layouts, on_device(): jnp.zeros((3, whole_body), jnp.float32).at[:, local_index]  4.36 us
    unnamed x24, local copies, waits for them, and re-layouts  3.43 us
    gather x6, local copies, waits for them, and re-layouts, one_slot(): picked = jnp.take(ext_blocks, source_ids, axis=1)  3.3 us
  transfers between devices with their start and end apart: 2, of which 0 were waited for; matrix products, arithmetic and copies ran while one was open for 1% of the time, Pallas kernels for 0%

commit v1 on v0

v1 whole, which is shorter than its diff:
```python
import functools
import math

import jax
import jax.numpy as jnp
from jax import lax
from jax.experimental import pallas as pl
from jax.experimental.pallas import tpu as pltpu
from jax.sharding import PartitionSpec as P

TILE = 128
SUB = 8
SCALE = 1.0 / (8.0 * math.pi)
MESH = pl.DeviceIdType.MESH


def pair_terms(x1, x2, x3, src):
    y1, y2, h, f1, f2, f3, h2 = src
    d1 = x1 - y1
    d2 = x2 - y2
    d3 = x3 - h
    r3 = x3 + h
    s = d1 * d1 + d2 * d2
    w = lax.rsqrt(s + d3 * d3 + 1.0)
    p = lax.rsqrt(s + r3 * r3)
    w3 = w * w * w
    p2 = p * p
    p3 = p2 * p
    along = d1 * f1 + d2 * f2
    full = along + d3 * f3
    mirror = along - r3 * f3
    cp3 = (h2 * x3) * p3
    alpha = (w + w3) - (p + cp3)
    gamma = 3.0 * (cp3 * p2) * mirror
    both = full * (w3 - p3) + gamma
    return (
        f1 * alpha + d1 * both,
        f2 * alpha + d2 * both,
        f3 * alpha + d3 * both + h2 * gamma,
    )


def kernel(
    n_region,
    n_member,
    pb,
    pos_hbm,
    force_hbm,
    plate_hbm,
    rank_hbm,
    owner_ref,
    list_ref,
    count_ref,
    pre_hbm,
    vel_out,
    body_out,
    pos,
    force,
    plate,
    rank,
    pre,
    ext,
    tgt,
    acc,
    vel,
    hot,
    in_sem,
    send_sem,
    recv_sem,
    vsend_sem,
    vrecv_sem,
):
    r = lax.axis_index("region")
    m = lax.axis_index("member")
    half = n_member // 2
    tiles = pos.shape[1] // TILE
    blobs = pos.shape[1]
    plates = owner_ref.shape[0]
    own_plates = pre.shape[0]
    pairs = list_ref.shape[1]
    has_low = r > 0
    has_high = r < n_region - 1
    to_high = jnp.logical_and(m >= half, has_high)
    to_low = jnp.logical_and(m < half, has_low)

    loads = [
        pltpu.make_async_copy(a, b, in_sem.at[i])
        for i, (a, b) in enumerate(
            ((pos_hbm, pos), (force_hbm, force), (plate_hbm, plate), (rank_hbm, rank), (pre_hbm, pre))
        )
    ]
    for load in loads:
        load.start()

    barrier = pltpu.get_barrier_semaphore()
    for step in range(1, n_member):
        pl.semaphore_signal(
            barrier, inc=1, device_id=(r, lax.rem(m + step, n_member)), device_id_type=MESH
        )

    @pl.when(has_low)
    def _():
        for k in range(half):
            pl.semaphore_signal(barrier, inc=1, device_id=(r - 1, half + k), device_id_type=MESH)

    @pl.when(has_high)
    def _():
        for k in range(half):
            pl.semaphore_signal(barrier, inc=1, device_id=(r + 1, k), device_id_type=MESH)

    for load in loads[:4]:
        load.wait()

    base = (half + m) * tiles
    plate_row = plate[...]
    rank_row = rank[...]
    live = plate_row < plates
    slot_of = jnp.zeros_like(plate_row)
    for k in range(plates):
        slot_of = jnp.where(plate_row == k, owner_ref[k], slot_of)
    body_at = jnp.where(live, slot_of * pb + rank_row, plates * pb).astype(jnp.float32)
    live_f = live.astype(jnp.float32)
    packed = jnp.concatenate(
        [pos[...], force[...] * live_f, body_at, jnp.zeros_like(body_at)], axis=0
    )
    for t in range(tiles):
        ext[base + t] = packed[:, t * TILE : (t + 1) * TILE]

    @pl.when(jnp.logical_not(has_low))
    def _():
        ext[pl.ds(0, half * tiles)] = jnp.zeros((half * tiles, SUB, TILE), jnp.float32)

    @pl.when(jnp.logical_not(has_high))
    def _():
        ext[pl.ds((half + n_member) * tiles, half * tiles)] = jnp.zeros(
            (half * tiles, SUB, TILE), jnp.float32
        )

    for t in range(tiles):
        for c in range(3):
            row = packed[c : c + 1, t * TILE : (t + 1) * TILE]
            tgt[t * 3 + c] = jnp.broadcast_to(row, (TILE, TILE)).T

    def block(e):
        return ext.at[pl.ds(e * tiles, tiles)]

    def near_copy(step):
        return pltpu.make_async_remote_copy(
            src_ref=block(half + m),
            dst_ref=block(half + m),
            send_sem=send_sem.at[step],
            recv_sem=recv_sem.at[half + m],
            device_id=(r, lax.rem(m + step, n_member)),
            device_id_type=MESH,
        )

    def rim_copy(k, shift, e):
        return pltpu.make_async_remote_copy(
            src_ref=block(half + m),
            dst_ref=block(e),
            send_sem=send_sem.at[n_member + k],
            recv_sem=recv_sem.at[e],
            device_id=(r + shift, lax.rem(m + k, n_member)),
            device_id_type=MESH,
        )

    def arrival(e):
        return pltpu.make_async_remote_copy(
            src_ref=block(e),
            dst_ref=block(e),
            send_sem=send_sem.at[0],
            recv_sem=recv_sem.at[e],
            device_id=(r, lax.rem(m + 1, n_member)),
            device_id_type=MESH,
        )

    rim_sends = jnp.where(jnp.logical_or(to_high, to_low), n_member, 0)
    pl.semaphore_wait(barrier, n_member - 1 + rim_sends)

    @pl.when(to_high)
    def _():
        for k in range(n_member):
            rim_copy(k, 1, m - half).start()

    @pl.when(to_low)
    def _():
        for k in range(n_member):
            rim_copy(k, -1, half + n_member + m).start()

    for step in range(1, n_member):
        near_copy(step).start()

    def one_pair(t, s, tile_id, first):
        keep = jnp.where(s < count_ref[t], SCALE, 0.0)
        rows = ext[tile_id]

        def wide(c):
            return jnp.broadcast_to(rows[c : c + 1], (SUB, TILE))

        h = wide(2)
        src = (wide(0), wide(1), h, wide(3) * keep, wide(4) * keep, wide(5) * keep, h + h)
        for b in range(TILE // SUB):
            at = pl.ds(b * SUB, SUB)
            terms = pair_terms(tgt[t * 3, at], tgt[t * 3 + 1, at], tgt[t * 3 + 2, at], src)
            for c in range(3):
                if first:
                    acc[t * 3 + c, at] = terms[c]
                else:
                    acc[t * 3 + c, at] = acc[t * 3 + c, at] + terms[c]

    @pl.loop(0, tiles)
    def _(t):
        one_pair(t, 0, base + t, True)

    for step in range(1, n_member):
        arrival(half + lax.rem(m + step, n_member)).wait_recv()

    @pl.when(has_low)
    def _():
        for k in range(half):
            arrival(k).wait_recv()

    @pl.when(has_high)
    def _():
        for k in range(half):
            arrival(half + n_member + k).wait_recv()

    @pl.loop(0, tiles * (pairs - 1))
    def _(i):
        t = i // (pairs - 1)
        s = i % (pairs - 1) + 1
        one_pair(t, s, list_ref[t, s], False)

    zeros = jnp.zeros((SUB - 3, TILE), jnp.float32)
    mine = pl.multiple_of(m * blobs, TILE)
    for t in range(tiles):
        rows = [jnp.sum(acc[t * 3 + c].T, axis=0, keepdims=True) for c in range(3)]
        at = pl.multiple_of(mine + t * TILE, TILE)
        vel[:, pl.ds(at, TILE)] = jnp.concatenate(rows + [zeros], axis=0)
        for c in range(3):
            vel_out[c : c + 1, t * TILE : (t + 1) * TILE] = rows[c]

    def vel_copy(step, at):
        part = vel.at[:, pl.ds(pl.multiple_of(at * blobs, TILE), blobs)]
        return pltpu.make_async_remote_copy(
            src_ref=part,
            dst_ref=part,
            send_sem=vsend_sem.at[step],
            recv_sem=vrecv_sem.at[at],
            device_id=(r, lax.rem(m + step, n_member)),
            device_id_type=MESH,
        )

    for step in range(1, n_member):
        vel_copy(step, m).start()

    width = hot.shape[0] // own_plates
    place = lax.broadcasted_iota(jnp.int32, (hot.shape[0], TILE), 0)

    @pl.loop(0, n_member * tiles)
    def _(i):
        local = ext[half * tiles + i][6:7].astype(jnp.int32) - m * (own_plates * pb)
        row = jnp.full_like(local, -1)
        for k in range(own_plates):
            inside = jnp.logical_and(local >= k * pb, local < (k + 1) * pb)
            row = jnp.where(inside, local + k * (width - pb), row)
        at = pl.multiple_of(i * TILE, TILE)
        hot[:, pl.ds(at, TILE)] = jnp.where(place == row, 1.0, 0.0).astype(jnp.bfloat16)

    loads[4].wait()
    for step in range(1, n_member):
        vel_copy(step, lax.rem(m + step, n_member)).wait_recv()

    placed = lax.dot_general(
        vel[...].astype(jnp.bfloat16),
        hot[...],
        (((1,), (1,)), ((), ())),
        preferred_element_type=jnp.float32,
    )
    order = pre.shape[2]
    total = 2 * width
    for k in range(own_plates):
        part = placed[:, k * width : (k + 1) * width]
        part = jnp.concatenate([part, jnp.zeros((SUB, total - width), jnp.float32)], axis=1)
        body = part[0:1]
        for c in range(1, 3):
            body = body + pltpu.roll(part, c * pb, 1)[c : c + 1]
        body_out[k : k + 1] = lax.dot_general(
            body[:, :order].astype(jnp.bfloat16),
            pre[k],
            (((1,), (1,)), ((), ())),
            preferred_element_type=jnp.float32,
        )

    for step in range(1, n_member):
        near_copy(step).wait_send()
        vel_copy(step, m).wait_send()

    @pl.when(to_high)
    def _():
        for k in range(n_member):
            rim_copy(k, 1, m - half).wait_send()

    @pl.when(to_low)
    def _():
        for k in range(n_member):
            rim_copy(k, -1, half + n_member + m).wait_send()


def on_device(n_region, n_member, positions, forces, blob_platelet, blob_rank, owner, pair_list, pair_count, pre):
    blobs = positions.shape[1]
    tiles = blobs // TILE
    own_plates, order, _ = pre.shape
    pb = order // 3
    width = -(-pb // TILE) * TILE
    anywhere = pl.BlockSpec(memory_space=pl.ANY)
    scalars = pl.BlockSpec(memory_space=pltpu.SMEM)
    vector = pl.BlockSpec(memory_space=pltpu.VMEM)
    return pl.pallas_call(
        functools.partial(kernel, n_region, n_member, pb),
        out_shape=(
            jax.ShapeDtypeStruct((3, blobs), jnp.float32),
            jax.ShapeDtypeStruct((own_plates, order), jnp.float32),
        ),
        in_specs=[anywhere] * 4 + [scalars] * 3 + [anywhere],
        out_specs=(vector, vector),
        scratch_shapes=[
            pltpu.VMEM((3, blobs), jnp.float32),
            pltpu.VMEM((3, blobs), jnp.float32),
            pltpu.VMEM((1, blobs), jnp.int32),
            pltpu.VMEM((1, blobs), jnp.int32),
            pltpu.VMEM(pre.shape, pre.dtype),
            pltpu.VMEM((2 * n_member * tiles, SUB, TILE), jnp.float32),
            pltpu.VMEM((3 * tiles, TILE, TILE), jnp.float32),
            pltpu.VMEM((3 * tiles, TILE, TILE), jnp.float32),
            pltpu.VMEM((SUB, n_member * blobs), jnp.float32),
            pltpu.VMEM((own_plates * width, n_member * blobs), jnp.bfloat16),
            pltpu.SemaphoreType.DMA((5,)),
            pltpu.SemaphoreType.DMA((2 * n_member,)),
            pltpu.SemaphoreType.DMA((2 * n_member,)),
            pltpu.SemaphoreType.DMA((n_member,)),
            pltpu.SemaphoreType.DMA((n_member,)),
        ],
        compiler_params=pltpu.CompilerParams(collective_id=0, has_side_effects=True),
    )(
        positions,
        forces,
        blob_platelet.reshape(1, blobs),
        blob_rank.reshape(1, blobs),
        owner,
        pair_list,
        pair_count,
        pre,
    )


def solution(mesh):
    placed = (
        P(None, ("region", "member")),
        P(None, ("region", "member")),
        P(("region", "member")),
        P(("region", "member")),
        P("region"),
        P(("region", "member"), None),
        P(("region", "member")),
        P(("region", "member"), None, None),
    )
    return jax.shard_map(
        functools.partial(on_device, mesh.shape["region"], mesh.shape["member"]),
        mesh=mesh,
        in_specs=placed,
        out_specs=(P(None, ("region", "member")), P(("region", "member"), None)),
        check_vma=False,
    )
```

time: 66.8 us -> 22.7 us (0.34)
  blocking collectives: 31.2 us -> 0 us
  Pallas kernels: 0 us -> 15.8 us
  other arithmetic: 11.9 us -> 0 us
  local copies, waits for them, and re-layouts: 12.4 us -> 6.04 us
  loops' own time: 5.28 us -> 0 us
  starting transfers between devices: 4.32 us -> 0 us
    all_gather x3 -> x0, blocking collectives: 31.2 us -> none  [the longest x1 13.4 us: on_device(): lax.all_gather(blob_velocity, 'member', axis=1, tiled=True)]
    pallas_call x0 -> x1, Pallas kernels: none -> 15.8 us  [on_device(): pl.pallas_call(functools.partial(kernel, n_region, n_member, pb), out_sha...]
    reduce_sum x13 -> x0, other arithmetic: 8.77 us -> none  [the longest x6 6.11 us: stokes_sum(): return jnp.sum(direct + wall_term, axis=3)]
    another operation x1 -> x0, loops' own time: 5.28 us -> none  [on_device(): lax.fori_loop(0, pair_rounds, one_slot, jnp.zeros(targets.shape, jnp.floa...]
    scatter x1 -> x0, local copies, waits for them, and re-layouts: 4.36 us -> none  [on_device(): jnp.zeros((3, whole_body), jnp.float32).at[:, local_index]]
    ppermute x2 -> x0, starting transfers between devices: 4.32 us -> none  [the longest x1 3.03 us: padded(): lax.ppermute(tail, axis, [(i, (i + 1) % count) for i in range(ends)])]
    gather x6 -> x0, local copies, waits for them, and re-layouts: 3.3 us -> none  [one_slot(): picked = jnp.take(ext_blocks, source_ids, axis=1)]
    reshape x0 -> x2, local copies, waits for them, and re-layouts: none -> 1.81 us  [the longest x1 1.25 us: on_device(): blob_platelet.reshape(1, blobs)]
  transfers between devices with their start and end apart: 2 -> 0, of which waited for: 0 -> 0; matrix products, arithmetic and copies ran while one was open for 1% -> 0% of each run, Pallas kernels for 0% -> 0%
where the time goes in v1:
time: 22.7 us; the launch traced here: 22.5 us
  Pallas kernels  15.8 us (70%)
  local copies, waits for them, and re-layouts  6.04 us (27%)
  between operations  0.66 us (3%)
    pallas_call x1, Pallas kernels, on_device(): pl.pallas_call(functools.partial(kernel, n_region, n_member, pb), out_sha...  15.8 us
    unnamed x7, local copies, waits for them, and re-layouts  4.22 us
    reshape x1, local copies, waits for them, and re-layouts, on_device(): blob_platelet.reshape(1, blobs)  1.25 us
    reshape x1, local copies, waits for them, and re-layouts, on_device(): blob_rank.reshape(1, blobs)  0.56 us

profile of v1, /device:TPU:0, one launch (start us, length us, event | category | flops | bytes accessed | tf_op | source)
XLA Modules:
  0.0 22.5 jit_solution(3332162962402333266)
XLA Ops:
  0.6 0.0 copy-start.1
  0.6 1.3 %reshape.10.plate_hbm = s32[1,384]{1,0:T(1,128)} reshape(s32[384]{0:T(512)} %param.10) | data formatting | bytes 3072 | tf_op jit(solution)/shard_map/reshape | solution.py:348
  1.9 0.0 copy-done.1
  1.9 0.6 %reshape.11.rank_hbm = s32[1,384]{1,0:T(1,128)} reshape(s32[384]{0:T(512)S(1)} %copy-done.1) | data formatting | bytes 3072 | tf_op jit(solution)/shard_map/reshape | solution.py:349
  2.5 2.3 %copy.10.pre_hbm = bf16[2,486,486]{2,1,0:T(8,128)(2,1)} copy(bf16[2,486,486]{2,0,1:T(2,128)(2,1)} %param.15) | data formatting | bytes 1889568 | tf_op args[7]
  4.8 15.8 %shard_map.95 = (f32[3,384]{1,0:T(4,128)}, f32[2,486]{1,0:T(2,128)}) custom-call(f32[3,384]{1,0:T(4,128)} %pos_hbm.1, f32[3,384]{1,0:T(4,128)} %force_hbm.1, s32[1,384]{1,0:T(1,128)} %reshape.10.plate_hbm, s32[1,384]{1,0:T(1,128)} %reshape.11.rank_hbm, s32[8]{0:T(128)} %owner_ref.1, s32[3,8]{1,0:T(4,128)} %list_ref.1, s32[3]{0:T(128)} %count_ref.1, ...), custom_call_target="tpu_custom_call" | custom-call | tf_op jit(solution)/shard_map/pallas_call | solution.py:319
  20.6 0.0 copy-start
  20.6 1.3 %copy.13 = f32[3,384]{1,0:T(4,128)} copy(f32[3,384]{1,0:T(4,128)} %get-tuple-element.4) | data formatting | bytes 9216
  21.9 0.0 copy-done
  21.9 0.6 %copy.14 = f32[2,486]{1,0:T(2,128)} copy(f32[2,486]{1,0:T(2,128)S(1)} %copy-done) | data formatting | bytes 7776
Async XLA Ops:
  0.6 1.3 %copy-start.1 = (s32[384]{0:T(512)S(1)}, s32[384]{0:T(512)}, u32[]{:S(2)}) copy-start(s32[384]{0:T(512)} %param.11) | copy-start | bytes 4612
  20.6 1.3 %copy-start = (f32[2,486]{1,0:T(2,128)S(1)}, f32[2,486]{1,0:T(2,128)}, u32[]{:S(2)}) copy-start(f32[2,486]{1,0:T(2,128)} %get-tuple-element.5) | copy-start | bytes 11668

commit v2 on v1

--- a/solution.py
+++ b/solution.py
@@ -44,21 +44,23 @@
     n_region,
     n_member,
     pb,
+    own_plates,
     pos_hbm,
     force_hbm,
     plate_hbm,
     rank_hbm,
-    owner_ref,
-    list_ref,
-    count_ref,
-    pre_hbm,
+    owner_hbm,
+    list_hbm,
+    count_hbm,
     vel_out,
     body_out,
     pos,
     force,
     plate,
     rank,
-    pre,
+    owner_ref,
+    list_ref,
+    count_ref,
     ext,
     tgt,
     acc,
@@ -76,7 +78,6 @@
     tiles = pos.shape[1] // TILE
     blobs = pos.shape[1]
     plates = owner_ref.shape[0]
-    own_plates = pre.shape[0]
     pairs = list_ref.shape[1]
     has_low = r > 0
     has_high = r < n_region - 1
@@ -86,7 +87,8 @@
     loads = [
         pltpu.make_async_copy(a, b, in_sem.at[i])
         for i, (a, b) in enumerate(
-            ((pos_hbm, pos), (force_hbm, force), (plate_hbm, plate), (rank_hbm, rank), (pre_hbm, pre))
+            ((pos_hbm, pos), (force_hbm, force), (plate_hbm, plate.at[0]), (rank_hbm, rank.at[0]),
+             (owner_hbm, owner_ref), (list_hbm, list_ref), (count_hbm, count_ref))
         )
     ]
     for load in loads:
@@ -108,7 +110,7 @@
         for k in range(half):
             pl.semaphore_signal(barrier, inc=1, device_id=(r + 1, k), device_id_type=MESH)
 
-    for load in loads[:4]:
+    for load in loads:
         load.wait()
 
     base = (half + m) * tiles
@@ -237,8 +239,7 @@
         rows = [jnp.sum(acc[t * 3 + c].T, axis=0, keepdims=True) for c in range(3)]
         at = pl.multiple_of(mine + t * TILE, TILE)
         vel[:, pl.ds(at, TILE)] = jnp.concatenate(rows + [zeros], axis=0)
-        for c in range(3):
-            vel_out[c : c + 1, t * TILE : (t + 1) * TILE] = rows[c]
+        vel_out[:, t * TILE : (t + 1) * TILE] = jnp.concatenate(rows + [zeros], axis=0)
 
     def vel_copy(step, at):
         part = vel.at[:, pl.ds(pl.multiple_of(at * blobs, TILE), blobs)]
@@ -267,7 +268,6 @@
         at = pl.multiple_of(i * TILE, TILE)
         hot[:, pl.ds(at, TILE)] = jnp.where(place == row, 1.0, 0.0).astype(jnp.bfloat16)
 
-    loads[4].wait()
     for step in range(1, n_member):
         vel_copy(step, lax.rem(m + step, n_member)).wait_recv()
 
@@ -277,7 +277,7 @@
         (((1,), (1,)), ((), ())),
         preferred_element_type=jnp.float32,
     )
-    order = pre.shape[2]
+    order = 3 * pb
     total = 2 * width
     for k in range(own_plates):
         part = placed[:, k * width : (k + 1) * width]
@@ -285,12 +285,7 @@
         body = part[0:1]
         for c in range(1, 3):
             body = body + pltpu.roll(part, c * pb, 1)[c : c + 1]
-        body_out[k : k + 1] = lax.dot_general(
-            body[:, :order].astype(jnp.bfloat16),
-            pre[k],
-            (((1,), (1,)), ((), ())),
-            preferred_element_type=jnp.float32,
-        )
+        body_out[k : k + 1] = body[:, :order]
 
     for step in range(1, n_member):
         near_copy(step).wait_send()
@@ -313,29 +308,30 @@
     own_plates, order, _ = pre.shape
     pb = order // 3
     width = -(-pb // TILE) * TILE
-    anywhere = pl.BlockSpec(memory_space=pl.ANY)
-    scalars = pl.BlockSpec(memory_space=pltpu.SMEM)
+    far = pl.BlockSpec(memory_space=pltpu.HBM)
     vector = pl.BlockSpec(memory_space=pltpu.VMEM)
-    return pl.pallas_call(
-        functools.partial(kernel, n_region, n_member, pb),
+    velocity, body_in = pl.pallas_call(
+        functools.partial(kernel, n_region, n_member, pb, own_plates),
         out_shape=(
-            jax.ShapeDtypeStruct((3, blobs), jnp.float32),
-            jax.ShapeDtypeStruct((own_plates, order), jnp.float32),
+            pltpu.VMEM((SUB, blobs), jnp.float32),
+            pltpu.VMEM((own_plates, order), jnp.float32),
         ),
-        in_specs=[anywhere] * 4 + [scalars] * 3 + [anywhere],
+        in_specs=[far] * 7,
         out_specs=(vector, vector),
         scratch_shapes=[
             pltpu.VMEM((3, blobs), jnp.float32),
             pltpu.VMEM((3, blobs), jnp.float32),
             pltpu.VMEM((1, blobs), jnp.int32),
             pltpu.VMEM((1, blobs), jnp.int32),
-            pltpu.VMEM(pre.shape, pre.dtype),
+            pltpu.SMEM(owner.shape, jnp.int32),
+            pltpu.SMEM(pair_list.shape, jnp.int32),
+            pltpu.SMEM(pair_count.shape, jnp.int32),
             pltpu.VMEM((2 * n_member * tiles, SUB, TILE), jnp.float32),
             pltpu.VMEM((3 * tiles, TILE, TILE), jnp.float32),
             pltpu.VMEM((3 * tiles, TILE, TILE), jnp.float32),
             pltpu.VMEM((SUB, n_member * blobs), jnp.float32),
             pltpu.VMEM((own_plates * width, n_member * blobs), jnp.bfloat16),
-            pltpu.SemaphoreType.DMA((5,)),
+            pltpu.SemaphoreType.DMA((7,)),
             pltpu.SemaphoreType.DMA((2 * n_member,)),
             pltpu.SemaphoreType.DMA((2 * n_member,)),
             pltpu.SemaphoreType.DMA((n_member,)),
@@ -345,13 +341,16 @@
     )(
         positions,
         forces,
-        blob_platelet.reshape(1, blobs),
-        blob_rank.reshape(1, blobs),
+        blob_platelet,
+        blob_rank,
         owner,
         pair_list,
         pair_count,
-        pre,
-    )
+    )
+    body_velocity = jnp.einsum(
+        "pab,pb->pa", pre, body_in.astype(jnp.bfloat16), preferred_element_type=jnp.float32
+    )
+    return velocity[:3], body_velocity
 
 
 def solution(mesh):

time: 22.7 us -> 16.6 us (0.73)
  local copies, waits for them, and re-layouts: 6.04 us -> 1.22 us
  Pallas kernels: 15.8 us -> 14.2 us
  matrix products: 0 us -> 0.36 us
    unnamed x7 -> x2, local copies, waits for them, and re-layouts: 4.22 us -> 0.01 us
    reshape x2 -> x0, local copies, waits for them, and re-layouts: 1.81 us -> none  [the longest x1 1.25 us: on_device(): blob_platelet.reshape(1, blobs)]
    pallas_call x1, Pallas kernels: 15.8 us -> 14.2 us  [on_device(): pl.pallas_call(functools.partial(kernel, n_region, n_member, pb, own_plat...]
    dot_general x0 -> x1, local copies, waits for them, and re-layouts: none -> 0.61 us  [on_device(): jnp.einsum('pab,pb->pa', pre, body_in.astype(jnp.bfloat16), preferred_ele...]
    slice x0 -> x1, local copies, waits for them, and re-layouts: none -> 0.6 us  [on_device(): return (velocity[:3], body_velocity)]
    dot_general x0 -> x1, matrix products: none -> 0.36 us  [on_device(): jnp.einsum('pab,pb->pa', pre, body_in.astype(jnp.bfloat16), preferred_ele...]
where the time goes in v2:
time: 16.6 us; the launch traced here: 16.4 us
  Pallas kernels  14.2 us (86%)
  local copies, waits for them, and re-layouts  1.22 us (7%)
  between operations  0.65 us (4%)
  matrix products  0.36 us (2%)
    pallas_call x1, Pallas kernels, on_device(): pl.pallas_call(functools.partial(kernel, n_region, n_member, pb, own_plat...  14.2 us
    dot_general x1, local copies, waits for them, and re-layouts, on_device(): jnp.einsum('pab,pb->pa', pre, body_in.astype(jnp.bfloat16), preferred_ele...  0.61 us
    slice x1, local copies, waits for them, and re-layouts, on_device(): return (velocity[:3], body_velocity)  0.6 us
    dot_general x1, matrix products, on_device(): jnp.einsum('pab,pb->pa', pre, body_in.astype(jnp.bfloat16), preferred_ele...  0.36 us

profile of v2, /device:TPU:0, one launch (start us, length us, event | category | flops | bytes accessed | tf_op | source)
XLA Modules:
  0.0 16.4 jit_solution(2181499312081181542)
XLA Ops:
  0.6 0.0 copy-start
  0.6 14.2 %shard_map.95 = (f32[8,384]{1,0:T(8,128)S(1)}, f32[2,486]{1,0:T(2,128)S(1)}) custom-call(f32[3,384]{1,0:T(4,128)} %pos_hbm.1, f32[3,384]{1,0:T(4,128)} %force_hbm.1, s32[384]{0:T(512)} %plate_hbm.1, s32[384]{0:T(512)} %rank_hbm.1, s32[8]{0:T(128)} %owner_hbm.1, s32[3,8]{1,0:T(4,128)} %list_hbm.1, s32[3]{0:T(128)} %count_hbm.1), custom_call_target="tpu_custom_call" | custom-call | tf_op jit(solution)/shard_map/pallas_call | solution.py:313
  14.9 0.6 %slice.3 = f32[3,384]{1,0:T(4,128)} slice(f32[8,384]{1,0:T(8,128)S(1)} %get-tuple-element.4), slice={[0:3], [0:384]} | slice | bytes 9216 | tf_op jit(solution)/shard_map/slice | solution.py:353
  15.5 0.0 copy-done
  15.5 0.4 %fusion = f32[2,1,486]{2,1,0:T(1,128)S(1)} fusion(bf16[2,486,486]{2,0,1:T(2,128)(2,1)S(1)} %copy-done, bf16[2,486,1]{1,0,2:T(2,128)(2,1)S(1)} %convert_bitcast_fusion), kind=kOutput, calls=%fused_computation | convolution fusion | flops 944784 | bytes 950616 | tf_op jit(solution)/shard_map/pab,pb->pa/dot_general | solution.py:350
  15.8 0.6 %copy.18 = f32[2,1,486]{2,0,1:T(2,128)} copy(f32[2,1,486]{2,1,0:T(1,128)S(1)} %fusion) | data formatting | bytes 7776 | tf_op jit(solution)/shard_map/pab,pb->pa/dot_general | solution.py:350
  (1 shorter events, 0.0 us)
Async XLA Ops:
  0.6 14.8 %copy-start = (bf16[2,486,486]{2,0,1:T(2,128)(2,1)S(1)}, bf16[2,486,486]{2,0,1:T(2,128)(2,1)}, u32[]{:S(2)}) copy-start(bf16[2,486,486]{2,0,1:T(2,128)(2,1)} %param.15) | copy-start | bytes 2834356

commit v3 on v2

--- a/solution.py
+++ b/solution.py
@@ -10,6 +10,7 @@
 
 TILE = 128
 SUB = 8
+VROWS = 4
 SCALE = 1.0 / (8.0 * math.pi)
 MESH = pl.DeviceIdType.MESH
 
@@ -227,33 +228,31 @@
         for k in range(half):
             arrival(half + n_member + k).wait_recv()
 
-    @pl.loop(0, tiles * (pairs - 1))
-    def _(i):
-        t = i // (pairs - 1)
-        s = i % (pairs - 1) + 1
-        one_pair(t, s, list_ref[t, s], False)
-
-    zeros = jnp.zeros((SUB - 3, TILE), jnp.float32)
-    mine = pl.multiple_of(m * blobs, TILE)
-    for t in range(tiles):
-        rows = [jnp.sum(acc[t * 3 + c].T, axis=0, keepdims=True) for c in range(3)]
-        at = pl.multiple_of(mine + t * TILE, TILE)
-        vel[:, pl.ds(at, TILE)] = jnp.concatenate(rows + [zeros], axis=0)
-        vel_out[:, t * TILE : (t + 1) * TILE] = jnp.concatenate(rows + [zeros], axis=0)
-
-    def vel_copy(step, at):
-        part = vel.at[:, pl.ds(pl.multiple_of(at * blobs, TILE), blobs)]
+    zeros = jnp.zeros((VROWS - 3, TILE), jnp.float32)
+
+    def vel_copy(t, step, at):
+        part = vel.at[:, pl.ds(pl.multiple_of(at * blobs + t * TILE, TILE), TILE)]
         return pltpu.make_async_remote_copy(
             src_ref=part,
             dst_ref=part,
-            send_sem=vsend_sem.at[step],
-            recv_sem=vrecv_sem.at[at],
+            send_sem=vsend_sem.at[t, step],
+            recv_sem=vrecv_sem.at[t, at],
             device_id=(r, lax.rem(m + step, n_member)),
             device_id_type=MESH,
         )
 
-    for step in range(1, n_member):
-        vel_copy(step, m).start()
+    for t in range(tiles):
+
+        @pl.loop(1, pairs)
+        def _(s):
+            one_pair(t, s, list_ref[t, s], False)
+
+        rows = [jnp.sum(acc[t * 3 + c].T, axis=0, keepdims=True) for c in range(3)]
+        at = pl.multiple_of(m * blobs + t * TILE, TILE)
+        vel[:, pl.ds(at, TILE)] = jnp.concatenate(rows + [zeros], axis=0)
+        vel_out[:, t * TILE : (t + 1) * TILE] = jnp.concatenate(rows, axis=0)
+        for step in range(1, n_member):
+            vel_copy(t, step, m).start()
 
     width = hot.shape[0] // own_plates
     place = lax.broadcasted_iota(jnp.int32, (hot.shape[0], TILE), 0)
@@ -269,7 +268,8 @@
         hot[:, pl.ds(at, TILE)] = jnp.where(place == row, 1.0, 0.0).astype(jnp.bfloat16)
 
     for step in range(1, n_member):
-        vel_copy(step, lax.rem(m + step, n_member)).wait_recv()
+        for t in range(tiles):
+            vel_copy(t, step, lax.rem(m + step, n_member)).wait_recv()
 
     placed = lax.dot_general(
         vel[...].astype(jnp.bfloat16),
@@ -281,7 +281,7 @@
     total = 2 * width
     for k in range(own_plates):
         part = placed[:, k * width : (k + 1) * width]
-        part = jnp.concatenate([part, jnp.zeros((SUB, total - width), jnp.float32)], axis=1)
+        part = jnp.concatenate([part, jnp.zeros((VROWS, total - width), jnp.float32)], axis=1)
         body = part[0:1]
         for c in range(1, 3):
             body = body + pltpu.roll(part, c * pb, 1)[c : c + 1]
@@ -289,7 +289,8 @@
 
     for step in range(1, n_member):
         near_copy(step).wait_send()
-        vel_copy(step, m).wait_send()
+        for t in range(tiles):
+            vel_copy(t, step, m).wait_send()
 
     @pl.when(to_high)
     def _():
@@ -313,7 +314,7 @@
     velocity, body_in = pl.pallas_call(
         functools.partial(kernel, n_region, n_member, pb, own_plates),
         out_shape=(
-            pltpu.VMEM((SUB, blobs), jnp.float32),
+            pltpu.VMEM((3, blobs), jnp.float32),
             pltpu.VMEM((own_plates, order), jnp.float32),
         ),
         in_specs=[far] * 7,
@@ -329,13 +330,13 @@
             pltpu.VMEM((2 * n_member * tiles, SUB, TILE), jnp.float32),
             pltpu.VMEM((3 * tiles, TILE, TILE), jnp.float32),
             pltpu.VMEM((3 * tiles, TILE, TILE), jnp.float32),
-            pltpu.VMEM((SUB, n_member * blobs), jnp.float32),
+            pltpu.VMEM((VROWS, n_member * blobs), jnp.float32),
             pltpu.VMEM((own_plates * width, n_member * blobs), jnp.bfloat16),
             pltpu.SemaphoreType.DMA((7,)),
             pltpu.SemaphoreType.DMA((2 * n_member,)),
             pltpu.SemaphoreType.DMA((2 * n_member,)),
-            pltpu.SemaphoreType.DMA((n_member,)),
-            pltpu.SemaphoreType.DMA((n_member,)),
+            pltpu.SemaphoreType.DMA((tiles, n_member)),
+            pltpu.SemaphoreType.DMA((tiles, n_member)),
         ],
         compiler_params=pltpu.CompilerParams(collective_id=0, has_side_effects=True),
     )(
@@ -350,7 +351,7 @@
     body_velocity = jnp.einsum(
         "pab,pb->pa", pre, body_in.astype(jnp.bfloat16), preferred_element_type=jnp.float32
     )
-    return velocity[:3], body_velocity
+    return velocity, body_velocity
 
 
 def solution(mesh):

time: 16.6 us -> 16.6 us (level)
    slice x1 -> x0, local copies, waits for them, and re-layouts: 0.6 us -> none  [on_device(): return (velocity[:3], body_velocity)]
    unnamed x2 -> x3, local copies, waits for them, and re-layouts: 0.01 us -> 0.61 us
where the time goes in v3:
time: 16.6 us; the launch traced here: 16.5 us
  Pallas kernels  14.3 us (86%)
  local copies, waits for them, and re-layouts  1.22 us (7%)
  between operations  0.65 us (4%)
  matrix products  0.36 us (2%)
    pallas_call x1, Pallas kernels, on_device(): pl.pallas_call(functools.partial(kernel, n_region, n_member, pb, own_plat...  14.3 us
    dot_general x1, local copies, waits for them, and re-layouts, on_device(): jnp.einsum('pab,pb->pa', pre, body_in.astype(jnp.bfloat16), preferred_ele...  0.61 us
    unnamed x3, local copies, waits for them, and re-layouts  0.61 us
    dot_general x1, matrix products, on_device(): jnp.einsum('pab,pb->pa', pre, body_in.astype(jnp.bfloat16), preferred_ele...  0.36 us

profile of v3, /device:TPU:0, one launch (start us, length us, event | category | flops | bytes accessed | tf_op | source)
XLA Modules:
  0.0 16.5 jit_solution(5408314153902659741)
XLA Ops:
  0.6 0.0 copy-start
  0.6 14.3 %shard_map.95 = (f32[3,384]{1,0:T(4,128)S(1)}, f32[2,486]{1,0:T(2,128)S(1)}) custom-call(f32[3,384]{1,0:T(4,128)} %pos_hbm.1, f32[3,384]{1,0:T(4,128)} %force_hbm.1, s32[384]{0:T(512)} %plate_hbm.1, s32[384]{0:T(512)} %rank_hbm.1, s32[8]{0:T(128)} %owner_hbm.1, s32[3,8]{1,0:T(4,128)} %list_hbm.1, s32[3]{0:T(128)} %count_hbm.1), custom_call_target="tpu_custom_call" | custom-call | tf_op jit(solution)/shard_map/pallas_call | solution.py:314
  14.9 0.6 %copy.20 = f32[3,384]{1,0:T(4,128)} copy(f32[3,384]{1,0:T(4,128)S(1)} %get-tuple-element.6) | data formatting | bytes 9216
  15.5 0.0 copy-done
  15.5 0.4 %fusion = f32[2,1,486]{2,1,0:T(1,128)S(1)} fusion(bf16[2,486,486]{2,0,1:T(2,128)(2,1)S(1)} %copy-done, bf16[2,486,1]{1,0,2:T(2,128)(2,1)S(1)} %convert_bitcast_fusion), kind=kOutput, calls=%fused_computation | convolution fusion | flops 944784 | bytes 950616 | tf_op jit(solution)/shard_map/pab,pb->pa/dot_general | solution.py:351
  15.9 0.6 %copy.18 = f32[2,1,486]{2,0,1:T(2,128)} copy(f32[2,1,486]{2,1,0:T(1,128)S(1)} %fusion) | data formatting | bytes 7776 | tf_op jit(solution)/shard_map/pab,pb->pa/dot_general | solution.py:351
  (1 shorter events, 0.0 us)
Async XLA Ops:
  0.6 14.9 %copy-start = (bf16[2,486,486]{2,0,1:T(2,128)(2,1)S(1)}, bf16[2,486,486]{2,0,1:T(2,128)(2,1)}, u32[]{:S(2)}) copy-start(bf16[2,486,486]{2,0,1:T(2,128)(2,1)} %param.15) | copy-start | bytes 2834356

commit v4 on v3

--- a/solution.py
+++ b/solution.py
@@ -301,6 +301,11 @@
     def _():
         for k in range(n_member):
             rim_copy(k, -1, half + n_member + m).wait_send()
+
+
+def finish(vel_ref, body_ref, vel_out, body_out):
+    vel_out[...] = vel_ref[...]
+    body_out[...] = body_ref[...]
 
 
 def on_device(n_region, n_member, positions, forces, blob_platelet, blob_rank, owner, pair_list, pair_count, pre):
@@ -351,7 +356,16 @@
     body_velocity = jnp.einsum(
         "pab,pb->pa", pre, body_in.astype(jnp.bfloat16), preferred_element_type=jnp.float32
     )
-    return velocity, body_velocity
+    return pl.pallas_call(
+        finish,
+        out_shape=(
+            jax.ShapeDtypeStruct(velocity.shape, jnp.float32),
+            jax.ShapeDtypeStruct(body_velocity.shape, jnp.float32),
+        ),
+        in_specs=[vector, vector],
+        out_specs=(vector, vector),
+        compiler_params=pltpu.CompilerParams(vmem_limit_bytes=1024 * 1024),
+    )(velocity, body_velocity)
 
 
 def solution(mesh):

time: 16.6 us -> 16.1 us (0.970)
  local copies, waits for them, and re-layouts: 1.22 us -> 0.02 us
  Pallas kernels: 14.3 us -> 14.9 us
    pallas_call x0 -> x1, Pallas kernels: none -> 0.62 us  [on_device(): pl.pallas_call(finish, out_shape=(jax.ShapeDtypeStruct(velocity.shape, jn...]
    dot_general x1, local copies, waits for them, and re-layouts: 0.61 us -> 0.01 us  [on_device(): jnp.einsum('pab,pb->pa', pre, body_in.astype(jnp.bfloat16), preferred_ele...]
    unnamed x3 -> x2, local copies, waits for them, and re-layouts: 0.61 us -> 0.01 us
where the time goes in v4:
time: 16.1 us; the launch traced here: 15.9 us
  Pallas kernels  14.9 us (93%)
  between operations  0.67 us (4%)
  matrix products  0.36 us (2%)
    pallas_call x1, Pallas kernels, on_device(): pl.pallas_call(functools.partial(kernel, n_region, n_member, pb, own_plat...  14.3 us
    pallas_call x1, Pallas kernels, on_device(): pl.pallas_call(finish, out_shape=(jax.ShapeDtypeStruct(velocity.shape, jn...  0.62 us
    dot_general x1, matrix products, on_device(): jnp.einsum('pab,pb->pa', pre, body_in.astype(jnp.bfloat16), preferred_ele...  0.36 us

profile of v4, /device:TPU:0, one launch (start us, length us, event | category | flops | bytes accessed | tf_op | source)
XLA Modules:
  0.0 15.9 jit_solution(10304322933146483548)
XLA Ops:
  0.6 0.0 copy-start
  0.6 14.3 %shard_map.95 = (f32[3,384]{1,0:T(4,128)S(1)}, f32[2,486]{1,0:T(2,128)S(1)}) custom-call(f32[3,384]{1,0:T(4,128)} %pos_hbm.1, f32[3,384]{1,0:T(4,128)} %force_hbm.1, s32[384]{0:T(512)} %plate_hbm.1, s32[384]{0:T(512)} %rank_hbm.1, s32[8]{0:T(128)} %owner_hbm.1, s32[3,8]{1,0:T(4,128)} %list_hbm.1, s32[3]{0:T(128)} %count_hbm.1), custom_call_target="tpu_custom_call" | custom-call | tf_op jit(solution)/shard_map/pallas_call | solution.py:319
  14.9 0.0 copy-done
  14.9 0.4 %fusion = f32[2,1,486]{2,1,0:T(1,128)S(1)} fusion(bf16[2,486,486]{2,0,1:T(2,128)(2,1)S(1)} %copy-done, bf16[2,486,1]{1,0,2:T(2,128)(2,1)S(1)} %convert_bitcast_fusion), kind=kOutput, calls=%fused_computation | convolution fusion | flops 944784 | bytes 950616 | tf_op jit(solution)/shard_map/pab,pb->pa/dot_general | solution.py:356
  15.3 0.6 %shard_map.96 = (f32[3,384]{1,0:T(4,128)}, f32[2,486]{1,0:T(2,128)}) custom-call(f32[3,384]{1,0:T(4,128)S(1)} %get-tuple-element.4.vel_ref, f32[2,486]{1,0:T(2,128)S(1)} %bitcast.5), custom_call_target="tpu_custom_call" | custom-call | tf_op jit(solution)/shard_map/pallas_call | solution.py:359
  (2 shorter events, 0.0 us)
Async XLA Ops:
  0.6 14.3 %copy-start = (bf16[2,486,486]{2,0,1:T(2,128)(2,1)S(1)}, bf16[2,486,486]{2,0,1:T(2,128)(2,1)}, u32[]{:S(2)}) copy-start(bf16[2,486,486]{2,0,1:T(2,128)(2,1)} %param.15) | copy-start | bytes 2834356

commit v5 on v4

--- a/solution.py
+++ b/solution.py
@@ -241,12 +241,12 @@
             device_id_type=MESH,
         )
 
+    @pl.loop(0, tiles)
+    def _(t):
+        for s in range(1, pairs):
+            one_pair(t, s, list_ref[t, s], False)
+
     for t in range(tiles):
-
-        @pl.loop(1, pairs)
-        def _(s):
-            one_pair(t, s, list_ref[t, s], False)
-
         rows = [jnp.sum(acc[t * 3 + c].T, axis=0, keepdims=True) for c in range(3)]
         at = pl.multiple_of(m * blobs + t * TILE, TILE)
         vel[:, pl.ds(at, TILE)] = jnp.concatenate(rows + [zeros], axis=0)

time: 16.1 us -> 15.8 us (0.981)
  Pallas kernels: 14.9 us -> 14.6 us
    pallas_call x1, Pallas kernels: 14.3 us -> 14 us  [on_device(): pl.pallas_call(functools.partial(kernel, n_region, n_member, pb, own_plat...]
where the time goes in v5:
time: 15.8 us; the launch traced here: 15.7 us
  Pallas kernels  14.6 us (92%)
  between operations  0.67 us (4%)
  matrix products  0.36 us (2%)
    pallas_call x1, Pallas kernels, on_device(): pl.pallas_call(functools.partial(kernel, n_region, n_member, pb, own_plat...  14 us
    pallas_call x1, Pallas kernels, on_device(): pl.pallas_call(finish, out_shape=(jax.ShapeDtypeStruct(velocity.shape, jn...  0.62 us
    dot_general x1, matrix products, on_device(): jnp.einsum('pab,pb->pa', pre, body_in.astype(jnp.bfloat16), preferred_ele...  0.36 us

profile of v5, /device:TPU:0, one launch (start us, length us, event | category | flops | bytes accessed | tf_op | source)
XLA Modules:
  0.0 15.7 jit_solution(3029437716597162874)
XLA Ops:
  0.6 0.0 copy-start
  0.6 14.0 %shard_map.95 = (f32[3,384]{1,0:T(4,128)S(1)}, f32[2,486]{1,0:T(2,128)S(1)}) custom-call(f32[3,384]{1,0:T(4,128)} %pos_hbm.1, f32[3,384]{1,0:T(4,128)} %force_hbm.1, s32[384]{0:T(512)} %plate_hbm.1, s32[384]{0:T(512)} %rank_hbm.1, s32[8]{0:T(128)} %owner_hbm.1, s32[3,8]{1,0:T(4,128)} %list_hbm.1, s32[3]{0:T(128)} %count_hbm.1), custom_call_target="tpu_custom_call" | custom-call | tf_op jit(solution)/shard_map/pallas_call | solution.py:319
  14.7 0.0 copy-done
  14.7 0.4 %fusion = f32[2,1,486]{2,1,0:T(1,128)S(1)} fusion(bf16[2,486,486]{2,0,1:T(2,128)(2,1)S(1)} %copy-done, bf16[2,486,1]{1,0,2:T(2,128)(2,1)S(1)} %convert_bitcast_fusion), kind=kOutput, calls=%fused_computation | convolution fusion | flops 944784 | bytes 950616 | tf_op jit(solution)/shard_map/pab,pb->pa/dot_general | solution.py:356
  15.1 0.6 %shard_map.96 = (f32[3,384]{1,0:T(4,128)}, f32[2,486]{1,0:T(2,128)}) custom-call(f32[3,384]{1,0:T(4,128)S(1)} %get-tuple-element.4.vel_ref, f32[2,486]{1,0:T(2,128)S(1)} %bitcast.5), custom_call_target="tpu_custom_call" | custom-call | tf_op jit(solution)/shard_map/pallas_call | solution.py:359
  (2 shorter events, 0.0 us)
Async XLA Ops:
  0.6 14.1 %copy-start = (bf16[2,486,486]{2,0,1:T(2,128)(2,1)S(1)}, bf16[2,486,486]{2,0,1:T(2,128)(2,1)}, u32[]{:S(2)}) copy-start(bf16[2,486,486]{2,0,1:T(2,128)(2,1)} %param.15) | copy-start | bytes 2834356
